TPU v7x, 32 devices: a whole 2x2x4 slice. The times are simulated.
32 devices in a mesh: grp: 2 (over x), gx: 4 (over z), gy: 4 (over y, core).
Axes of the slice: x: 2, y: 2, z: 4, core: 2. Of those that a mesh axis runs over, the one named last changes fastest.
Arguments:
- theta_anomaly: float32 [192, 64, 128], P(('grp', 'gx'), 'gy'), may hold values from -4 to 4
- humidity_ratio: float32 [192, 64, 128], P(('grp', 'gx'), 'gy'), may hold values from 0.6 to 1.4
- zonal_velocity: float32 [192, 64, 128], P(('grp', 'gx'), 'gy'), may hold values from -1.8 to 1.8
- meridional_velocity: float32 [192, 64, 128], P(('grp', 'gx'), 'gy'), may hold values from -1.8 to 1.8
- vertical_velocity: float32 [192, 64, 128], P(('grp', 'gx'), 'gy'), may hold values from -1.8 to 1.8
- patch_processor_map: int32 [8, 4, 8], P(('grp', 'gx'), 'gy'), may hold values from 0 to 3, as said below
- particle_bucket_population: int32 [8, 4, 8], P(('grp', 'gx'), 'gy'), may hold values from 0 to 1024, as said below
- particle_size_quadratic: float32 [8, 4, 8, 1024], P(('grp', 'gx'), 'gy'), may hold values from 0.25 to 4
- represented_number: float32 [8, 4, 8, 1024], P(('grp', 'gx'), 'gy'), may hold values from 0.5 to 2
- particle_location_number: int32 [8, 4, 8, 1024], P(('grp', 'gx'), 'gy'), may hold values from 48 to 6095, as said below
Outputs:
- final_temperature: float32 [192, 64, 128], P(('grp', 'gx'), 'gy')
- final_vapour: float32 [192, 64, 128], P(('grp', 'gx'), 'gy')
- final_east: float32 [192, 64, 128], P(('grp', 'gx'), 'gy')
- final_north: float32 [192, 64, 128], P(('grp', 'gx'), 'gy')
- final_vertical: float32 [192, 64, 128], P(('grp', 'gx'), 'gy')
- final_size_quadratic: float32 [8, 4, 8, 1024], P(('grp', 'gx'), 'gy')
Inputs may be any that keep to these rules, and one draw needn't show every extreme that they name: `patch_processor_map`: entry [a, y, b] is the index along gx of the device in the same row (same grp half, same gy) that holds the droplets of column block b of device (a, y). Different blocks of one device go to different owners, so one device sends at most 2 blocks to one owner; in every row some owner holds 2 blocks from every device of the row. `particle_bucket_population`: entry [a, y, r] counts the live droplets of slot r = s x 2 + t of the owner (a, y); they are the first ones of the slot. A slot that receives no block has none; every slot of an owner that holds 2 blocks from every device is full. `particle_location_number`: the cell within the slot's block, column 128 + level, with levels from 48 to 79. Within a slot the live droplets are sorted by column, and so are the others.
All inputs are finite; a program needn't handle non-finite values.
Results may differ from a plain program's by a relative error of at most 0.0003.
Values sent between devices are 32-bit elements; how exact they have to be, the bound alone decides.
A program may use at most 64 MiB of HBM per device.

v0:
```python
import jax
import jax.numpy as jnp
from jax import lax
from jax.sharding import PartitionSpec as P

NBD = 8
NSUB = 4
ITERS = 4
TIME_INCREMENT = 0.15
THERMAL_LIFT = 0.5
HUMID_LIFT = 0.3
HELMHOLTZ = 0.001
CLAUSIUS_FACTOR = 0.2
GROWTH = 0.5
GROWTH_SLOPE = 0.1
SUB_STEP = 0.25
CURVATURE = 0.05
FLOOR_SQUARE = 0.04
CONDENSE = 0.2
PHASE_WARMING = 2.5


def with_halo(block, sides, width):
    for axis, dim in sides:
        count = lax.axis_size(axis)
        forward = [(i, i + 1) for i in range(count - 1)]
        forward.append((count - 1, 0))
        backward = [(target, source) for source, target in forward]
        low = lax.ppermute(
            lax.slice_in_dim(block, block.shape[dim] - width, None, axis=dim), axis, forward
        )
        high = lax.ppermute(lax.slice_in_dim(block, 0, width, axis=dim), axis, backward)
        block = jnp.concatenate([low, block, high], axis=dim)
    return block


def surround(stacked):
    return with_halo(stacked, ((("grp", "gx"), 1), ("gy", 2)), 1)


def beside(padded):
    return (
        padded[:, 2:, 1:-1, :],
        padded[:, :-2, 1:-1, :],
        padded[:, 1:-1, 2:, :],
        padded[:, 1:-1, :-2, :],
    )


def level_above(values):
    return jnp.concatenate([values[..., 1:], jnp.zeros_like(values[..., :1])], axis=-1)


def level_below(values):
    return jnp.concatenate([jnp.zeros_like(values[..., :1]), values[..., :-1]], axis=-1)


def profiles(layer_altitudes):
    heights = jnp.arange(layer_altitudes, dtype=jnp.float32)
    midpoint_mass_per_volume = jnp.exp(-(heights + 0.5) / layer_altitudes)
    interface_mass_per_volume = jnp.where(
        heights < layer_altitudes - 1, jnp.exp(-(heights + 1.0) / layer_altitudes), 0.0
    )
    return (midpoint_mass_per_volume, interface_mass_per_volume)


def operate(values, midpoint_mass_per_volume, interface_mass_per_volume):
    east_side, west_side, north_side, south_side = beside(surround(values[None]))
    return (
        midpoint_mass_per_volume
        * ((4.0 + HELMHOLTZ) * values - east_side[0] - west_side[0] - north_side[0] - south_side[0])
        + interface_mass_per_volume * (values - level_above(values))
        + level_below(interface_mass_per_volume) * (values - level_below(values))
    )


def both_sums(residual, applied):
    return lax.psum(
        (jnp.sum(residual * residual), jnp.sum(residual * applied)), ("grp", "gx", "gy")
    )


def solve_pressure(right_side, midpoint_mass_per_volume, interface_mass_per_volume):
    potential = jnp.zeros_like(right_side)
    residual = right_side
    applied = operate(residual, midpoint_mass_per_volume, interface_mass_per_volume)
    norm_now, product = both_sums(residual, applied)
    step_length = norm_now / product
    direction, along_dir = (residual, applied)
    for iteration in range(ITERS):
        potential = potential + step_length * direction
        residual = residual - step_length * along_dir
        if iteration + 1 < ITERS:
            applied = operate(residual, midpoint_mass_per_volume, interface_mass_per_volume)
            norm_next, product = both_sums(residual, applied)
            beta_ratio = norm_next / norm_now
            step_length = norm_next / (product - beta_ratio * norm_next / step_length)
            direction = residual + beta_ratio * direction
            along_dir = applied + beta_ratio * along_dir
            norm_now = norm_next
    return potential


def momentum_update(
    theta_anomaly,
    humidity_ratio,
    zonal_velocity,
    meridional_velocity,
    vertical_velocity,
    midpoint_mass_per_volume,
    interface_mass_per_volume,
):
    raised_airmass = vertical_velocity + TIME_INCREMENT * (
        THERMAL_LIFT * theta_anomaly + HUMID_LIFT * humidity_ratio
    )
    east_side, west_side, north_side, south_side = beside(
        surround(jnp.stack([zonal_velocity, meridional_velocity]))
    )
    divergence = midpoint_mass_per_volume * (
        (east_side[0] - west_side[0]) * 0.5 + (north_side[1] - south_side[1]) * 0.5
    ) + 0.5 * (
        level_above(midpoint_mass_per_volume * raised_airmass)
        - level_below(midpoint_mass_per_volume * raised_airmass)
    )
    potential = solve_pressure(
        -divergence / TIME_INCREMENT, midpoint_mass_per_volume, interface_mass_per_volume
    )
    pot_east, pot_west, pot_north, pot_south = beside(surround(potential[None]))
    zonal_velocity = zonal_velocity - TIME_INCREMENT * 0.5 * (pot_east[0] - pot_west[0])
    meridional_velocity = meridional_velocity - TIME_INCREMENT * 0.5 * (pot_north[0] - pot_south[0])
    vertical_velocity = raised_airmass - TIME_INCREMENT * 0.5 * (
        level_above(potential) - level_below(potential)
    )
    scalar_quantities = jnp.stack([theta_anomaly, humidity_ratio])
    tra_east, tra_west, tra_north, tra_south = beside(surround(scalar_quantities))
    lower_level = jnp.concatenate(
        [scalar_quantities[..., :1], scalar_quantities[..., :-1]], axis=-1
    )
    upper_level = jnp.concatenate(
        [scalar_quantities[..., 1:], scalar_quantities[..., -1:]], axis=-1
    )
    tendency = (
        jnp.maximum(zonal_velocity, 0.0) * (scalar_quantities - tra_west)
        + jnp.minimum(zonal_velocity, 0.0) * (tra_east - scalar_quantities)
        + jnp.maximum(meridional_velocity, 0.0) * (scalar_quantities - tra_south)
        + jnp.minimum(meridional_velocity, 0.0) * (tra_north - scalar_quantities)
        + jnp.maximum(vertical_velocity, 0.0) * (scalar_quantities - lower_level)
        + jnp.minimum(vertical_velocity, 0.0) * (upper_level - scalar_quantities)
    )
    moved = scalar_quantities - TIME_INCREMENT * tendency
    return (moved[0], moved[1], zonal_velocity, meridional_velocity, vertical_velocity)


def grow_droplets(supersat_ratio, warmth, particle_size_quadratic, represented_number, alive_mask):
    growth_rate = GROWTH * jnp.exp(GROWTH_SLOPE * warmth)
    square_now = particle_size_quadratic
    for substep in range(NSUB):
        square_now = jnp.maximum(
            square_now
            + 2.0 * SUB_STEP * growth_rate * (supersat_ratio - CURVATURE / jnp.sqrt(square_now)),
            FLOOR_SQUARE,
        )
    grown_square = jnp.where(alive_mask, square_now, particle_size_quadratic)
    mass_change = jnp.where(
        alive_mask,
        represented_number
        * (
            grown_square * jnp.sqrt(grown_square)
            - particle_size_quadratic * jnp.sqrt(particle_size_quadratic)
        ),
        0.0,
    )
    return (grown_square, mass_change)


def grow_rows(columns, radius_squared_rows, mult_rows, local_cell, alive_mask):
    row_count = columns.shape[0]
    thermal_couple = columns.reshape(row_count, 2, -1)
    cells_per = thermal_couple.shape[2]
    supersat_ratio = jnp.take_along_axis(thermal_couple[:, 0], local_cell, axis=1)
    warmth = jnp.take_along_axis(thermal_couple[:, 1], local_cell, axis=1)
    grown_square, mass_change = grow_droplets(
        supersat_ratio, warmth, radius_squared_rows, mult_rows, alive_mask
    )
    flat_cell = local_cell + cells_per * jnp.arange(row_count, dtype=jnp.int32)[:, None]
    liquid_content = CONDENSE * jax.ops.segment_sum(
        mass_change.reshape(-1), flat_cell.reshape(-1), num_segments=row_count * cells_per
    )
    return (grown_square, liquid_content.reshape(row_count, cells_per))


def into_patches(values):
    domain_length_east, domain_length_north, layer_depth = values.shape
    shaped = values.reshape(domain_length_east, NBD, domain_length_north // NBD, layer_depth)
    return shaped.transpose(1, 0, 2, 3).reshape(NBD, -1)


def from_blocks(blocks, domain_length_east, domain_length_north, layer_depth):
    shaped = blocks.reshape(NBD, domain_length_east, domain_length_north // NBD, layer_depth)
    return shaped.transpose(1, 0, 2, 3).reshape(
        domain_length_east, domain_length_north, layer_depth
    )


def routing_plan(owner_row, slots, row_count):
    row_index = jnp.arange(row_count, dtype=jnp.int32)[:, None]
    block_index = jnp.arange(owner_row.shape[0], dtype=jnp.int32)[None, :]
    matches = (owner_row[None, :] == row_index // slots) & (
        block_index % slots == row_index % slots
    )
    return matches.astype(jnp.float32)


def on_device(
    theta_anomaly,
    humidity_ratio,
    zonal_velocity,
    meridional_velocity,
    vertical_velocity,
    patch_processor_map,
    particle_bucket_population,
    particle_size_quadratic,
    represented_number,
    particle_location_number,
):
    domain_length_east, domain_length_north, layer_altitudes = theta_anomaly.shape
    midpoint_mass_per_volume, interface_mass_per_volume = profiles(layer_altitudes)
    radius_squared_rows = particle_size_quadratic[0, 0]
    mult_rows = represented_number[0, 0]
    cell_rows = particle_location_number[0, 0]
    count_rows = particle_bucket_population[0, 0]
    row_count = radius_squared_rows.shape[0]
    slots = row_count // lax.axis_size("gx")
    routing = routing_plan(patch_processor_map[0, 0], slots, row_count)
    layer_low = 0
    layer_depth = layer_altitudes - layer_low
    local_cell = (
        cell_rows // layer_altitudes * layer_depth + cell_rows % layer_altitudes - layer_low
    )
    alive_mask = (
        jnp.arange(radius_squared_rows.shape[1], dtype=jnp.int32)[None, :] < count_rows[:, None]
    )
    advected_theta, advected_humidity, zonal_velocity, meridional_velocity, vertical_velocity = (
        momentum_update(
            theta_anomaly,
            humidity_ratio,
            zonal_velocity,
            meridional_velocity,
            vertical_velocity,
            midpoint_mass_per_volume,
            interface_mass_per_volume,
        )
    )
    supersat_ratio = advected_humidity * jnp.exp(-CLAUSIUS_FACTOR * advected_theta) - 1.0
    thermal_couple = jnp.stack(
        [into_patches(supersat_ratio), into_patches(advected_theta)], axis=1
    ).reshape(NBD, -1)
    columns = jnp.dot(routing, thermal_couple, precision=lax.Precision.HIGHEST)
    arrived_columns = lax.all_to_all(columns, "gx", split_axis=0, concat_axis=0, tiled=True)
    radius_squared_rows, owner_rows = grow_rows(
        arrived_columns, radius_squared_rows, mult_rows, local_cell, alive_mask
    )
    condensed_rows = lax.all_to_all(owner_rows, "gx", split_axis=0, concat_axis=0, tiled=True)
    liquid_content = from_blocks(
        jnp.dot(routing.T, condensed_rows, precision=lax.Precision.HIGHEST),
        domain_length_east,
        domain_length_north,
        layer_depth,
    )
    theta_anomaly = advected_theta + PHASE_WARMING * liquid_content
    humidity_ratio = advected_humidity - liquid_content
    return (
        theta_anomaly,
        humidity_ratio,
        zonal_velocity,
        meridional_velocity,
        vertical_velocity,
        radius_squared_rows[None, None],
    )


def solution(mesh):
    placed = (
        P(("grp", "gx"), "gy", None),
        P(("grp", "gx"), "gy", None),
        P(("grp", "gx"), "gy", None),
        P(("grp", "gx"), "gy", None),
        P(("grp", "gx"), "gy", None),
        P(("grp", "gx"), "gy", None),
        P(("grp", "gx"), "gy", None),
        P(("grp", "gx"), "gy", None, None),
        P(("grp", "gx"), "gy", None, None),
        P(("grp", "gx"), "gy", None, None),
    )
    return jax.shard_map(
        on_device,
        mesh=mesh,
        in_specs=placed,
        out_specs=(
            P(("grp", "gx"), "gy", None),
            P(("grp", "gx"), "gy", None),
            P(("grp", "gx"), "gy", None),
            P(("grp", "gx"), "gy", None),
            P(("grp", "gx"), "gy", None),
            P(("grp", "gx"), "gy", None, None),
        ),
        check_vma=False,
    )
```

profile of v0, /device:TPU:0, one launch (start us, length us, event | category | flops | bytes accessed | tf_op | source)
XLA Modules:
  0.0 446.6 jit_solution(3342073956511347936)
XLA Ops:
  1.5 6.0 %collective-permute-start = (f32[2,1,16,128]{3,2,1,0:T(8,128)S(1)}, f32[2,1,16,128]{3,2,1,0:T(8,128)S(1)}, u32[]{:S(2)}, u32[]{:S(2)}) collective-permute-start(f32[2,1,16,128]{3,2,1,0:T(8,128)S(1)} %get-tuple-element.59), channel_id=1, source_target_pairs={{4,0},{8,4},{12,8},{16,12},{20,16},{24,20},{28,24},{0,28},{5,1},{9... | collective-permute-start | bytes 49160 | tf_op jit(solution)/shard_map/ppermute | solution.py:32
  8.3 4.7 %collective-permute-start.23 = (f32[2,1,16,128]{3,1,2,0:T(1,128)}, f32[2,1,16,128]{3,1,2,0:T(1,128)}, u32[]{:S(2)}, u32[]{:S(2)}) collective-permute-start(f32[2,1,16,128]{3,1,2,0:T(1,128)} %get-tuple-element.65), channel_id=1, source_target_pairs={{4,0},{8,4},{12,8},{16,12},{20,16},{24,20},{28,24},{0,28},{5,1},{9... | collective-permute-start | bytes 49160 | tf_op jit(solution)/shard_map/ppermute | solution.py:32
  18.4 2.0 collective-permute-start.4
  22.1 4.7 %collective-permute-done.5 = f32[1,1,16,128]{3,2,1,0:T(8,128)S(1)} collective-permute-done((f32[1,1,16,128]{3,2,1,0:T(8,128)S(1)}, f32[1,1,16,128]{3,2,1,0:T(8,128)S(1)}, u32[]{:S(2)}, u32[]{:S(2)}) %collective-permute-start.5) | collective-permute-done | bytes 8224 | tf_op jit(solution)/shard_map/ppermute | solution.py:29
  30.8 37.1 %all-reduce.15 = (f32[]{:T(128)}, f32[]{:T(128)}) all-reduce(f32[]{:T(128)} %get-tuple-element.26, f32[]{:T(128)} %get-tuple-element.25), channel_id=1, replica_groups=mesh['grp'=2,'gx'=4,'gy'=4] {'grp','gx','gy'}, use_global_device_ids=true, to_apply=%region_1.2 | all-reduce | flops 2 | bytes 16 | tf_op jit(solution)/shard_map/psum | solution.py:78
  69.3 4.0 collective-permute-start.8
  74.7 5.0 %collective-permute-done.9 = f32[1,1,16,128]{3,2,1,0:T(8,128)S(1)} collective-permute-done((f32[1,1,16,128]{3,2,1,0:T(8,128)S(1)}, f32[1,1,16,128]{3,2,1,0:T(8,128)S(1)}, u32[]{:S(2)}, u32[]{:S(2)}) %collective-permute-start.9) | collective-permute-done | bytes 8224 | tf_op jit(solution)/shard_map/ppermute | solution.py:29
  83.8 37.2 %all-reduce.14 = (f32[]{:T(128)}, f32[]{:T(128)}) all-reduce(f32[]{:T(128)} %get-tuple-element.24, f32[]{:T(128)} %get-tuple-element.23), channel_id=1, replica_groups=mesh['grp'=2,'gx'=4,'gy'=4] {'grp','gx','gy'}, use_global_device_ids=true, to_apply=%region_5.6 | all-reduce | flops 2 | bytes 16 | tf_op jit(solution)/shard_map/psum | solution.py:78
  125.7 4.0 collective-permute-start.12
  131.9 4.2 collective-permute-done.13
  141.0 37.2 %all-reduce.13 = (f32[]{:T(128)}, f32[]{:T(128)}) all-reduce(f32[]{:T(128)} %get-tuple-element.22, f32[]{:T(128)} %get-tuple-element.21), channel_id=1, replica_groups=mesh['grp'=2,'gx'=4,'gy'=4] {'grp','gx','gy'}, use_global_device_ids=true, to_apply=%region_9.10 | all-reduce | flops 2 | bytes 16 | tf_op jit(solution)/shard_map/psum | solution.py:78
  183.0 4.0 collective-permute-start.16
  190.1 3.3 collective-permute-done.17
  194.9 2.2 collective-permute-done.19
  197.9 37.4 %all-reduce.12 = (f32[]{:T(128)}, f32[]{:T(128)}) all-reduce(f32[]{:T(128)} %get-tuple-element.20, f32[]{:T(128)} %get-tuple-element.19), channel_id=1, replica_groups=mesh['grp'=2,'gx'=4,'gy'=4] {'grp','gx','gy'}, use_global_device_ids=true, to_apply=%region_13.14 | all-reduce | flops 2 | bytes 16 | tf_op jit(solution)/shard_map/psum | solution.py:78
  239.5 4.0 collective-permute-start.20
  244.8 5.0 %collective-permute-done.21 = f32[1,1,16,128]{3,2,1,0:T(8,128)S(1)} collective-permute-done((f32[1,1,16,128]{3,2,1,0:T(8,128)S(1)}, f32[1,1,16,128]{3,2,1,0:T(8,128)S(1)}, u32[]{:S(2)}, u32[]{:S(2)}) %collective-permute-start.21) | collective-permute-done | bytes 8224 | tf_op jit(solution)/shard_map/ppermute | solution.py:29
  258.6 3.8 all-to-all-start
  262.8 11.6 %all-to-all-done = f32[4,2,12288]{2,1,0:T(2,128)S(1)} async-done(((f32[4,2,12288]{2,1,0:T(2,128)}), f32[4,2,12288]{2,1,0:T(2,128)S(1)}, u32[]{:S(2)}, u32[]{:S(2)}) %all-to-all-start) | async-done | bytes 393248 | tf_op jit(solution)/shard_map/all_to_all | solution.py:259
  275.3 50.0 %gather_fusion = f32[8192]{0:T(1024)S(1)} fusion(f32[8,6144]{1,0:T(8,128)S(1)} %bitcast.262, s32[8192]{0:T(1024)S(1)} %bitcast.263), kind=kCustom, calls=%fused_computation.clone | custom fusion | bytes 131072 | tf_op jit(solution)/shard_map/jit(take_along_axis)/gather | solution.py:181
  325.5 50.0 %gather_fusion.1 = f32[8192]{0:T(1024)S(1)} fusion(f32[8,6144]{1,0:T(8,128)S(1)} %bitcast.261, s32[8192]{0:T(1024)S(1)} %bitcast.264), kind=kCustom, calls=%fused_computation.1.clone | custom fusion | bytes 131072 | tf_op jit(solution)/shard_map/jit(take_along_axis)/gather | solution.py:180
  376.3 56.7 %scatter_custom_fusion = f32[49152]{0:T(1024)S(1)} fusion(s32[8192]{0:T(1024)S(1)} %bitcast.293, f32[8192]{0:T(1024)S(1)} %bitcast.294, f32[]{:T(128)} %constant.107.clone.1), kind=kCustom, calls=%fused_computation.191 | custom fusion | flops 8192 | bytes 196612 | tf_op jit(solution)/shard_map/scatter-add | solution.py:186
  433.9 3.5 all-to-all-start.1
  437.4 7.3 %all-to-all-done.1 = f32[4,2,6144]{2,1,0:T(2,128)S(1)} async-done(((f32[4,2,6144]{2,1,0:T(2,128)}), f32[4,2,6144]{2,1,0:T(2,128)S(1)}, u32[]{:S(2)}, u32[]{:S(2)}) %all-to-all-start.1) | async-done | bytes 196640 | tf_op jit(solution)/shard_map/all_to_all | solution.py:263
  (189 shorter events, 46.5 us)
Async XLA Ops:
  1.5 13.0 %collective-permute-start = (f32[2,1,16,128]{3,2,1,0:T(8,128)S(1)}, f32[2,1,16,128]{3,2,1,0:T(8,128)S(1)}, u32[]{:S(2)}, u32[]{:S(2)}) collective-permute-start(f32[2,1,16,128]{3,2,1,0:T(8,128)S(1)} %get-tuple-element.59), channel_id=1, source_target_pairs={{4,0},{8,4},{12,8},{16,12},{20,16},{24,20},{28,24},{0,28},{5,1},{9... | collective-permute-start | bytes 49160 | tf_op jit(solution)/shard_map/ppermute | solution.py:32
  7.5 7.0 %collective-permute-start.1 = (f32[2,1,16,128]{3,2,1,0:T(8,128)S(1)}, f32[2,1,16,128]{3,2,1,0:T(8,128)S(1)}, u32[]{:S(2)}, u32[]{:S(2)}) collective-permute-start(f32[2,1,16,128]{3,2,1,0:T(8,128)S(1)} %get-tuple-element.58), channel_id=1, source_target_pairs={{0,4},{4,8},{8,12},{12,16},{16,20},{20,24},{24,28},{28,0},{1,5},{5... | collective-permute-start | bytes 49160 | tf_op jit(solution)/shard_map/ppermute | solution.py:29
  8.2 178.8 %collective-permute-start.22 = (f32[2,1,16,128]{3,1,2,0:T(1,128)}, f32[2,1,16,128]{3,1,2,0:T(1,128)S(1)}, u32[]{:S(2)}, u32[]{:S(2)}) collective-permute-start(f32[2,1,16,128]{3,1,2,0:T(1,128)} %get-tuple-element.64), channel_id=1, source_target_pairs={{0,4},{4,8},{8,12},{12,16},{16,20},{20,24},{24,28},{28,0},{1,5},{5... | collective-permute-start | bytes 49160 | tf_op jit(solution)/shard_map/ppermute | solution.py:29
  8.3 178.8 %collective-permute-start.23 = (f32[2,1,16,128]{3,1,2,0:T(1,128)}, f32[2,1,16,128]{3,1,2,0:T(1,128)}, u32[]{:S(2)}, u32[]{:S(2)}) collective-permute-start(f32[2,1,16,128]{3,1,2,0:T(1,128)} %get-tuple-element.65), channel_id=1, source_target_pairs={{4,0},{8,4},{12,8},{16,12},{20,16},{24,20},{28,24},{0,28},{5,1},{9... | collective-permute-start | bytes 49160 | tf_op jit(solution)/shard_map/ppermute | solution.py:32
  14.7 3.5 collective-permute-start.3
  18.4 3.7 collective-permute-start.4
  20.4 6.3 %collective-permute-start.5 = (f32[1,1,16,128]{3,2,1,0:T(8,128)S(1)}, f32[1,1,16,128]{3,2,1,0:T(8,128)S(1)}, u32[]{:S(2)}, u32[]{:S(2)}) collective-permute-start(f32[1,1,16,128]{3,2,1,0:T(8,128)S(1)} %get-tuple-element.94), channel_id=1, source_target_pairs={{0,4},{4,8},{8,12},{12,16},{16,20},{20,24},{24,28},{28,0},{1,5},{5... | collective-permute-start | bytes 24584 | tf_op jit(solution)/shard_map/ppermute | solution.py:29
  26.9 3.2 collective-permute-start.7
  69.3 5.4 %collective-permute-start.8 = (f32[1,1,16,128]{3,2,1,0:T(8,128)S(1)}, f32[1,1,16,128]{3,2,1,0:T(8,128)S(1)}, u32[]{:S(2)}, u32[]{:S(2)}) collective-permute-start(f32[1,1,16,128]{3,2,1,0:T(8,128)S(1)} %get-tuple-element.91), channel_id=1, source_target_pairs={{4,0},{8,4},{12,8},{16,12},{20,16},{24,20},{28,24},{0,28},{5,1},{9... | collective-permute-start | bytes 24584 | tf_op jit(solution)/shard_map/ppermute | solution.py:32
  73.3 6.3 %collective-permute-start.9 = (f32[1,1,16,128]{3,2,1,0:T(8,128)S(1)}, f32[1,1,16,128]{3,2,1,0:T(8,128)S(1)}, u32[]{:S(2)}, u32[]{:S(2)}) collective-permute-start(f32[1,1,16,128]{3,2,1,0:T(8,128)S(1)} %get-tuple-element.90), channel_id=1, source_target_pairs={{0,4},{4,8},{8,12},{12,16},{16,20},{20,24},{24,28},{28,0},{1,5},{5... | collective-permute-start | bytes 24584 | tf_op jit(solution)/shard_map/ppermute | solution.py:29
  79.8 3.3 collective-permute-start.11
  125.7 6.2 %collective-permute-start.12 = (f32[1,1,16,128]{3,2,1,0:T(8,128)S(1)}, f32[1,1,16,128]{3,2,1,0:T(8,128)S(1)}, u32[]{:S(2)}, u32[]{:S(2)}) collective-permute-start(f32[1,1,16,128]{3,2,1,0:T(8,128)S(1)} %get-tuple-element.87), channel_id=1, source_target_pairs={{4,0},{8,4},{12,8},{16,12},{20,16},{24,20},{28,24},{0,28},{5,1},{9... | collective-permute-start | bytes 24584 | tf_op jit(solution)/shard_map/ppermute | solution.py:32
  129.7 6.3 %collective-permute-start.13 = (f32[1,1,16,128]{3,2,1,0:T(8,128)S(1)}, f32[1,1,16,128]{3,2,1,0:T(8,128)S(1)}, u32[]{:S(2)}, u32[]{:S(2)}) collective-permute-start(f32[1,1,16,128]{3,2,1,0:T(8,128)S(1)} %get-tuple-element.86), channel_id=1, source_target_pairs={{0,4},{4,8},{8,12},{12,16},{16,20},{20,24},{24,28},{28,0},{1,5},{5... | collective-permute-start | bytes 24584 | tf_op jit(solution)/shard_map/ppermute | solution.py:29
  136.2 3.3 collective-permute-start.15
  183.0 7.1 %collective-permute-start.16 = (f32[1,1,16,128]{3,2,1,0:T(8,128)S(1)}, f32[1,1,16,128]{3,2,1,0:T(8,128)S(1)}, u32[]{:S(2)}, u32[]{:S(2)}) collective-permute-start(f32[1,1,16,128]{3,2,1,0:T(8,128)S(1)} %get-tuple-element.85), channel_id=1, source_target_pairs={{4,0},{8,4},{12,8},{16,12},{20,16},{24,20},{28,24},{0,28},{5,1},{9... | collective-permute-start | bytes 24584 | tf_op jit(solution)/shard_map/ppermute | solution.py:32
  187.0 6.3 %collective-permute-start.17 = (f32[1,1,16,128]{3,2,1,0:T(8,128)S(1)}, f32[1,1,16,128]{3,2,1,0:T(8,128)S(1)}, u32[]{:S(2)}, u32[]{:S(2)}) collective-permute-start(f32[1,1,16,128]{3,2,1,0:T(8,128)S(1)} %get-tuple-element.84), channel_id=1, source_target_pairs={{0,4},{4,8},{8,12},{12,16},{16,20},{20,24},{24,28},{28,0},{1,5},{5... | collective-permute-start | bytes 24584 | tf_op jit(solution)/shard_map/ppermute | solution.py:29
  188.3 66.0 %collective-permute-start.26 = (f32[2,26,1,128]{3,1,2,0:T(8,128)}, f32[2,26,1,128]{3,1,2,0:T(8,128)}, u32[]{:S(2)}, u32[]{:S(2)}) collective-permute-start(f32[2,26,1,128]{3,1,2,0:T(8,128)} %get-tuple-element.52), channel_id=1, source_target_pairs={{0,1},{1,2},{2,3},{3,0},{4,5},{5,6},{6,7},{7,4},{8,9},{9,10},{10,1... | collective-permute-start | bytes 79880 | tf_op jit(solution)/shard_map/ppermute | solution.py:29
  188.4 66.0 %collective-permute-start.27 = (f32[2,26,1,128]{3,1,2,0:T(8,128)}, f32[2,26,1,128]{3,1,2,0:T(8,128)}, u32[]{:S(2)}, u32[]{:S(2)}) collective-permute-start(f32[2,26,1,128]{3,1,2,0:T(8,128)} %get-tuple-element.53), channel_id=1, source_target_pairs={{1,0},{2,1},{3,2},{0,3},{5,4},{6,5},{7,6},{4,7},{9,8},{10,9},{11,1... | collective-permute-start | bytes 79880 | tf_op jit(solution)/shard_map/ppermute | solution.py:32
  194.0 3.1 collective-permute-start.19
  239.5 5.4 %collective-permute-start.20 = (f32[1,1,16,128]{3,2,1,0:T(8,128)S(1)}, f32[1,1,16,128]{3,2,1,0:T(8,128)S(1)}, u32[]{:S(2)}, u32[]{:S(2)}) collective-permute-start(f32[1,1,16,128]{3,2,1,0:T(8,128)S(1)} %get-tuple-element.79), channel_id=1, source_target_pairs={{4,0},{8,4},{12,8},{16,12},{20,16},{24,20},{28,24},{0,28},{5,1},{9... | collective-permute-start | bytes 24584 | tf_op jit(solution)/shard_map/ppermute | solution.py:32
  243.5 6.3 %collective-permute-start.21 = (f32[1,1,16,128]{3,2,1,0:T(8,128)S(1)}, f32[1,1,16,128]{3,2,1,0:T(8,128)S(1)}, u32[]{:S(2)}, u32[]{:S(2)}) collective-permute-start(f32[1,1,16,128]{3,2,1,0:T(8,128)S(1)} %get-tuple-element.78), channel_id=1, source_target_pairs={{0,4},{4,8},{8,12},{12,16},{16,20},{20,24},{24,28},{28,0},{1,5},{5... | collective-permute-start | bytes 24584 | tf_op jit(solution)/shard_map/ppermute | solution.py:29
  249.9 3.3 collective-permute-start.25
  258.6 15.8 %all-to-all-start = ((f32[4,2,12288]{2,1,0:T(2,128)}), f32[4,2,12288]{2,1,0:T(2,128)S(1)}, u32[]{:S(2)}, u32[]{:S(2)}) async-start(f32[4,2,12288]{2,1,0:T(2,128)} %fusion.110), calls=%async_computation | async-start | bytes 786432 | tf_op jit(solution)/shard_map/all_to_all | solution.py:259
  433.9 10.8 %all-to-all-start.1 = ((f32[4,2,6144]{2,1,0:T(2,128)}), f32[4,2,6144]{2,1,0:T(2,128)S(1)}, u32[]{:S(2)}, u32[]{:S(2)}) async-start(f32[4,2,6144]{2,1,0:T(2,128)} %all_to_all.13), calls=%async_computation.1 | async-start | bytes 393216 | tf_op jit(solution)/shard_map/all_to_all | solution.py:263
  (38 other events, 620.8 us)
where the time goes:
time: 448 us; the launch traced here: 447 us
  blocking collectives  149 us (33%)
  local copies, waits for them, and re-layouts  109 us (24%)
  other arithmetic  69.3 us (15%)
  waiting for transfers between devices  61.6 us (14%)
  starting transfers between devices  40.9 us (9%)
  between operations  15.2 us (3%)
    psum x4, blocking collectives, both_sums(): lax.psum((jnp.sum(residual * residual), jnp.sum(residual * applied)), ('g...  149 us
    scatter-add x1, other arithmetic, grow_rows(): jax.ops.segment_sum(mass_change.reshape(-1), flat_cell.reshape(-1), num_s...  56.7 us
    gather x2, local copies, waits for them, and re-layouts, grow_rows(): warmth = jnp.take_along_axis(thermal_couple[:, 1], local_cell, axis=1)  50.1 us
    gather x2, local copies, waits for them, and re-layouts, grow_rows(): jnp.take_along_axis(thermal_couple[:, 0], local_cell, axis=1)  50.1 us
    ppermute x14, waiting for transfers between devices, with_halo(): lax.ppermute(lax.slice_in_dim(block, block.shape[dim] - width, None, axis...  33.7 us
    ppermute x14, starting transfers between devices, with_halo(): lax.ppermute(lax.slice_in_dim(block, 0, width, axis=dim), axis, backward)  31.1 us
    all_to_all x1, waiting for transfers between devices, on_device(): lax.all_to_all(columns, 'gx', split_axis=0, concat_axis=0, tiled=True)  11.6 us
  transfers between devices with their start and end apart: 30, of which 22 were waited for; matrix products, arithmetic and copies ran while one was open for 3% of the time, Pallas kernels for 0%

commit v1 on v0

--- a/solution.py
+++ b/solution.py
@@ -76,7 +76,8 @@
 
 def both_sums(residual, applied):
     return lax.psum(
-        (jnp.sum(residual * residual), jnp.sum(residual * applied)), ("grp", "gx", "gy")
+        lax.psum((jnp.sum(residual * residual), jnp.sum(residual * applied)), ("gx", "gy")),
+        axis_name="grp",
     )
 
 

time: 448 us -> 423 us (0.944)
  waiting for transfers between devices: 61.6 us -> 50.8 us
  starting transfers between devices: 40.9 us -> 33 us
  blocking collectives: 149 us -> 143 us
    psum x4, blocking collectives: 149 us -> 120 us  [both_sums(): lax.psum((jnp.sum(residual * residual), jnp.sum(residual * applied)), ('g...]
    psum x0 -> x4, blocking collectives: none -> 22.2 us  [both_sums(): lax.psum(lax.psum((jnp.sum(residual * residual), jnp.sum(residual * appli...]
    ppermute x14, starting transfers between devices: 31.1 us -> 15.2 us  [with_halo(): lax.ppermute(lax.slice_in_dim(block, 0, width, axis=dim), axis, backward)]
    ppermute x14, waiting for transfers between devices: 33.7 us -> 25.1 us  [with_halo(): lax.ppermute(lax.slice_in_dim(block, block.shape[dim] - width, None, axis...]
    ppermute x14, starting transfers between devices: 2.48 us -> 10.5 us  [with_halo(): lax.ppermute(lax.slice_in_dim(block, block.shape[dim] - width, None, axis...]
where the time goes in v1:
time: 423 us; the launch traced here: 422 us
  blocking collectives  143 us (34%)
  local copies, waits for them, and re-layouts  109 us (26%)
  other arithmetic  69.3 us (16%)
  waiting for transfers between devices  50.8 us (12%)
  starting transfers between devices  33 us (8%)
  between operations  14.9 us (4%)
    psum x4, blocking collectives, both_sums(): lax.psum((jnp.sum(residual * residual), jnp.sum(residual * applied)), ('g...  120 us
    scatter-add x1, other arithmetic, grow_rows(): jax.ops.segment_sum(mass_change.reshape(-1), flat_cell.reshape(-1), num_s...  56.7 us
    gather x2, local copies, waits for them, and re-layouts, grow_rows(): warmth = jnp.take_along_axis(thermal_couple[:, 1], local_cell, axis=1)  50.1 us
    gather x2, local copies, waits for them, and re-layouts, grow_rows(): jnp.take_along_axis(thermal_couple[:, 0], local_cell, axis=1)  50.1 us
    ppermute x14, waiting for transfers between devices, with_halo(): lax.ppermute(lax.slice_in_dim(block, block.shape[dim] - width, None, axis...  25.1 us
    psum x4, blocking collectives, both_sums(): lax.psum(lax.psum((jnp.sum(residual * residual), jnp.sum(residual * appli...  22.2 us
    ppermute x14, starting transfers between devices, with_halo(): lax.ppermute(lax.slice_in_dim(block, 0, width, axis=dim), axis, backward)  15.2 us
    ppermute x14, starting transfers between devices, with_halo(): lax.ppermute(lax.slice_in_dim(block, block.shape[dim] - width, None, axis...  10.5 us
  transfers between devices with their start and end apart: 30, of which 22 were waited for; matrix products, arithmetic and copies ran while one was open for 3% of the time, Pallas kernels for 0%

profile of v1, /device:TPU:0, one launch (start us, length us, event | category | flops | bytes accessed | tf_op | source)
XLA Modules:
  0.0 421.7 jit_solution(3716670785689220768)
XLA Ops:
  1.5 6.0 %collective-permute-start = (f32[2,1,16,128]{3,2,1,0:T(8,128)S(1)}, f32[2,1,16,128]{3,2,1,0:T(8,128)S(1)}, u32[]{:S(2)}, u32[]{:S(2)}) collective-permute-start(f32[2,1,16,128]{3,2,1,0:T(8,128)S(1)} %get-tuple-element.67), channel_id=1, source_target_pairs={{4,0},{8,4},{12,8},{16,12},{20,16},{24,20},{28,24},{0,28},{5,1},{9... | collective-permute-start | bytes 49160 | tf_op jit(solution)/shard_map/ppermute | solution.py:32
  8.3 4.7 %collective-permute-start.23 = (f32[2,1,16,128]{3,1,2,0:T(1,128)}, f32[2,1,16,128]{3,1,2,0:T(1,128)}, u32[]{:S(2)}, u32[]{:S(2)}) collective-permute-start(f32[2,1,16,128]{3,1,2,0:T(1,128)} %get-tuple-element.73), channel_id=1, source_target_pairs={{4,0},{8,4},{12,8},{16,12},{20,16},{24,20},{28,24},{0,28},{5,1},{9... | collective-permute-start | bytes 49160 | tf_op jit(solution)/shard_map/ppermute | solution.py:32
  18.4 2.0 collective-permute-start.4
  22.1 4.7 %collective-permute-done.5 = f32[1,1,16,128]{3,2,1,0:T(8,128)S(1)} collective-permute-done((f32[1,1,16,128]{3,2,1,0:T(8,128)S(1)}, f32[1,1,16,128]{3,2,1,0:T(8,128)S(1)}, u32[]{:S(2)}, u32[]{:S(2)}) %collective-permute-start.5) | collective-permute-done | bytes 8224 | tf_op jit(solution)/shard_map/ppermute | solution.py:29
  30.8 30.1 %all-reduce.15 = (f32[]{:T(128)}, f32[]{:T(128)}) all-reduce(f32[]{:T(128)} %get-tuple-element.26, f32[]{:T(128)} %get-tuple-element.25), channel_id=1, replica_groups=mesh['grp'=2,'gx'=4,'gy'=4] {'gx','gy'}, use_global_device_ids=true, to_apply=%region_1.2 | all-reduce | flops 2 | bytes 16 | tf_op jit(solution)/shard_map/psum | solution.py:79
  60.9 5.5 %all-reduce.19 = (f32[]{:T(128)}, f32[]{:T(128)}) all-reduce(f32[]{:T(128)} %get-tuple-element.33, f32[]{:T(128)} %get-tuple-element.34), channel_id=1, replica_groups=mesh['grp'=2,'gx'=4,'gy'=4] {'grp'}, use_global_device_ids=true, to_apply=%region_2.3 | all-reduce | flops 2 | bytes 16 | tf_op jit(solution)/shard_map/psum | solution.py:78
  71.6 2.8 collective-permute-done.9
  78.4 30.1 %all-reduce.14 = (f32[]{:T(128)}, f32[]{:T(128)}) all-reduce(f32[]{:T(128)} %get-tuple-element.24, f32[]{:T(128)} %get-tuple-element.23), channel_id=1, replica_groups=mesh['grp'=2,'gx'=4,'gy'=4] {'gx','gy'}, use_global_device_ids=true, to_apply=%region_7.8 | all-reduce | flops 2 | bytes 16 | tf_op jit(solution)/shard_map/psum | solution.py:79
  108.5 5.5 %all-reduce.18 = (f32[]{:T(128)}, f32[]{:T(128)}) all-reduce(f32[]{:T(128)} %get-tuple-element.31, f32[]{:T(128)} %get-tuple-element.32), channel_id=1, replica_groups=mesh['grp'=2,'gx'=4,'gy'=4] {'grp'}, use_global_device_ids=true, to_apply=%region_8.9 | all-reduce | flops 2 | bytes 16 | tf_op jit(solution)/shard_map/psum | solution.py:78
  123.0 2.2 collective-permute-done.13
  130.0 30.2 %all-reduce.13 = (f32[]{:T(128)}, f32[]{:T(128)}) all-reduce(f32[]{:T(128)} %get-tuple-element.22, f32[]{:T(128)} %get-tuple-element.21), channel_id=1, replica_groups=mesh['grp'=2,'gx'=4,'gy'=4] {'gx','gy'}, use_global_device_ids=true, to_apply=%region_13.14 | all-reduce | flops 2 | bytes 16 | tf_op jit(solution)/shard_map/psum | solution.py:79
  160.2 5.6 %all-reduce.17 = (f32[]{:T(128)}, f32[]{:T(128)}) all-reduce(f32[]{:T(128)} %get-tuple-element.29, f32[]{:T(128)} %get-tuple-element.30), channel_id=1, replica_groups=mesh['grp'=2,'gx'=4,'gy'=4] {'grp'}, use_global_device_ids=true, to_apply=%region_14.15 | all-reduce | flops 2 | bytes 16 | tf_op jit(solution)/shard_map/psum | solution.py:78
  170.5 2.0 collective-permute-start.17
  178.4 2.2 collective-permute-done.19
  181.5 30.1 %all-reduce.12 = (f32[]{:T(128)}, f32[]{:T(128)}) all-reduce(f32[]{:T(128)} %get-tuple-element.20, f32[]{:T(128)} %get-tuple-element.19), channel_id=1, replica_groups=mesh['grp'=2,'gx'=4,'gy'=4] {'gx','gy'}, use_global_device_ids=true, to_apply=%region_19.20 | all-reduce | flops 2 | bytes 16 | tf_op jit(solution)/shard_map/psum | solution.py:79
  211.6 5.5 %all-reduce.16 = (f32[]{:T(128)}, f32[]{:T(128)}) all-reduce(f32[]{:T(128)} %get-tuple-element.27, f32[]{:T(128)} %get-tuple-element.28), channel_id=1, replica_groups=mesh['grp'=2,'gx'=4,'gy'=4] {'grp'}, use_global_device_ids=true, to_apply=%region_20.21 | all-reduce | flops 2 | bytes 16 | tf_op jit(solution)/shard_map/psum | solution.py:78
  224.8 2.8 collective-permute-done.21
  236.3 3.8 all-to-all-start
  240.5 10.0 %all-to-all-done = f32[4,2,12288]{2,1,0:T(2,128)S(1)} async-done(((f32[4,2,12288]{2,1,0:T(2,128)}), f32[4,2,12288]{2,1,0:T(2,128)S(1)}, u32[]{:S(2)}, u32[]{:S(2)}) %all-to-all-start) | async-done | bytes 393248 | tf_op jit(solution)/shard_map/all_to_all | solution.py:260
  251.4 50.0 %gather_fusion = f32[8192]{0:T(1024)S(1)} fusion(f32[8,6144]{1,0:T(8,128)S(1)} %bitcast.262, s32[8192]{0:T(1024)S(1)} %bitcast.263), kind=kCustom, calls=%fused_computation.clone | custom fusion | bytes 131072 | tf_op jit(solution)/shard_map/jit(take_along_axis)/gather | solution.py:182
  301.6 50.0 %gather_fusion.1 = f32[8192]{0:T(1024)S(1)} fusion(f32[8,6144]{1,0:T(8,128)S(1)} %bitcast.261, s32[8192]{0:T(1024)S(1)} %bitcast.264), kind=kCustom, calls=%fused_computation.1.clone | custom fusion | bytes 131072 | tf_op jit(solution)/shard_map/jit(take_along_axis)/gather | solution.py:181
  352.4 56.7 %scatter_custom_fusion = f32[49152]{0:T(1024)S(1)} fusion(s32[8192]{0:T(1024)S(1)} %bitcast.293, f32[8192]{0:T(1024)S(1)} %bitcast.294, f32[]{:T(128)} %constant.107.clone.1), kind=kCustom, calls=%fused_computation.191 | custom fusion | flops 8192 | bytes 196612 | tf_op jit(solution)/shard_map/scatter-add | solution.py:187
  409.9 3.5 all-to-all-start.1
  413.5 6.2 %all-to-all-done.1 = f32[4,2,6144]{2,1,0:T(2,128)S(1)} async-done(((f32[4,2,6144]{2,1,0:T(2,128)}), f32[4,2,6144]{2,1,0:T(2,128)S(1)}, u32[]{:S(2)}, u32[]{:S(2)}) %all-to-all-start.1) | async-done | bytes 196640 | tf_op jit(solution)/shard_map/all_to_all | solution.py:264
  (193 shorter events, 54.3 us)
Async XLA Ops:
  1.5 13.0 %collective-permute-start = (f32[2,1,16,128]{3,2,1,0:T(8,128)S(1)}, f32[2,1,16,128]{3,2,1,0:T(8,128)S(1)}, u32[]{:S(2)}, u32[]{:S(2)}) collective-permute-start(f32[2,1,16,128]{3,2,1,0:T(8,128)S(1)} %get-tuple-element.67), channel_id=1, source_target_pairs={{4,0},{8,4},{12,8},{16,12},{20,16},{24,20},{28,24},{0,28},{5,1},{9... | collective-permute-start | bytes 49160 | tf_op jit(solution)/shard_map/ppermute | solution.py:32
  7.5 7.0 %collective-permute-start.1 = (f32[2,1,16,128]{3,2,1,0:T(8,128)S(1)}, f32[2,1,16,128]{3,2,1,0:T(8,128)S(1)}, u32[]{:S(2)}, u32[]{:S(2)}) collective-permute-start(f32[2,1,16,128]{3,2,1,0:T(8,128)S(1)} %get-tuple-element.66), channel_id=1, source_target_pairs={{0,4},{4,8},{8,12},{12,16},{16,20},{20,24},{24,28},{28,0},{1,5},{5... | collective-permute-start | bytes 49160 | tf_op jit(solution)/shard_map/ppermute | solution.py:29
  8.2 164.3 %collective-permute-start.22 = (f32[2,1,16,128]{3,1,2,0:T(1,128)}, f32[2,1,16,128]{3,1,2,0:T(1,128)S(1)}, u32[]{:S(2)}, u32[]{:S(2)}) collective-permute-start(f32[2,1,16,128]{3,1,2,0:T(1,128)} %get-tuple-element.72), channel_id=1, source_target_pairs={{0,4},{4,8},{8,12},{12,16},{16,20},{20,24},{24,28},{28,0},{1,5},{5... | collective-permute-start | bytes 49160 | tf_op jit(solution)/shard_map/ppermute | solution.py:29
  8.3 164.3 %collective-permute-start.23 = (f32[2,1,16,128]{3,1,2,0:T(1,128)}, f32[2,1,16,128]{3,1,2,0:T(1,128)}, u32[]{:S(2)}, u32[]{:S(2)}) collective-permute-start(f32[2,1,16,128]{3,1,2,0:T(1,128)} %get-tuple-element.73), channel_id=1, source_target_pairs={{4,0},{8,4},{12,8},{16,12},{20,16},{24,20},{28,24},{0,28},{5,1},{9... | collective-permute-start | bytes 49160 | tf_op jit(solution)/shard_map/ppermute | solution.py:32
  14.7 3.5 collective-permute-start.3
  18.4 3.7 collective-permute-start.4
  20.4 6.3 %collective-permute-start.5 = (f32[1,1,16,128]{3,2,1,0:T(8,128)S(1)}, f32[1,1,16,128]{3,2,1,0:T(8,128)S(1)}, u32[]{:S(2)}, u32[]{:S(2)}) collective-permute-start(f32[1,1,16,128]{3,2,1,0:T(8,128)S(1)} %get-tuple-element.102), channel_id=1, source_target_pairs={{0,4},{4,8},{8,12},{12,16},{16,20},{20,24},{24,28},{28,0},{1,5},{5... | collective-permute-start | bytes 24584 | tf_op jit(solution)/shard_map/ppermute | solution.py:29
  26.9 3.2 collective-permute-start.7
  67.9 3.7 collective-permute-start.8
  67.9 6.4 %collective-permute-start.9 = (f32[1,1,16,128]{3,2,1,0:T(8,128)S(1)}, f32[1,1,16,128]{3,2,1,0:T(8,128)S(1)}, u32[]{:S(2)}, u32[]{:S(2)}) collective-permute-start(f32[1,1,16,128]{3,2,1,0:T(8,128)S(1)} %get-tuple-element.98), channel_id=1, source_target_pairs={{0,4},{4,8},{8,12},{12,16},{16,20},{20,24},{24,28},{28,0},{1,5},{5... | collective-permute-start | bytes 24584 | tf_op jit(solution)/shard_map/ppermute | solution.py:29
  74.4 3.2 collective-permute-start.11
  118.7 4.3 %collective-permute-start.12 = (f32[1,1,16,128]{3,2,1,0:T(8,128)S(1)}, f32[1,1,16,128]{3,2,1,0:T(8,128)S(1)}, u32[]{:S(2)}, u32[]{:S(2)}) collective-permute-start(f32[1,1,16,128]{3,2,1,0:T(8,128)S(1)} %get-tuple-element.95), channel_id=1, source_target_pairs={{4,0},{8,4},{12,8},{16,12},{20,16},{24,20},{28,24},{0,28},{5,1},{9... | collective-permute-start | bytes 24584 | tf_op jit(solution)/shard_map/ppermute | solution.py:32
  118.8 6.4 %collective-permute-start.13 = (f32[1,1,16,128]{3,2,1,0:T(8,128)S(1)}, f32[1,1,16,128]{3,2,1,0:T(8,128)S(1)}, u32[]{:S(2)}, u32[]{:S(2)}) collective-permute-start(f32[1,1,16,128]{3,2,1,0:T(8,128)S(1)} %get-tuple-element.94), channel_id=1, source_target_pairs={{0,4},{4,8},{8,12},{12,16},{16,20},{20,24},{24,28},{28,0},{1,5},{5... | collective-permute-start | bytes 24584 | tf_op jit(solution)/shard_map/ppermute | solution.py:29
  125.3 3.2 collective-permute-start.15
  170.4 5.1 %collective-permute-start.16 = (f32[1,1,16,128]{3,2,1,0:T(8,128)S(1)}, f32[1,1,16,128]{3,2,1,0:T(8,128)S(1)}, u32[]{:S(2)}, u32[]{:S(2)}) collective-permute-start(f32[1,1,16,128]{3,2,1,0:T(8,128)S(1)} %get-tuple-element.93), channel_id=1, source_target_pairs={{4,0},{8,4},{12,8},{16,12},{20,16},{24,20},{28,24},{0,28},{5,1},{9... | collective-permute-start | bytes 24584 | tf_op jit(solution)/shard_map/ppermute | solution.py:32
  170.5 6.4 %collective-permute-start.17 = (f32[1,1,16,128]{3,2,1,0:T(8,128)S(1)}, f32[1,1,16,128]{3,2,1,0:T(8,128)S(1)}, u32[]{:S(2)}, u32[]{:S(2)}) collective-permute-start(f32[1,1,16,128]{3,2,1,0:T(8,128)S(1)} %get-tuple-element.92), channel_id=1, source_target_pairs={{0,4},{4,8},{8,12},{12,16},{16,20},{20,24},{24,28},{28,0},{1,5},{5... | collective-permute-start | bytes 24584 | tf_op jit(solution)/shard_map/ppermute | solution.py:29
  173.8 58.2 %collective-permute-start.26 = (f32[2,26,1,128]{3,1,2,0:T(8,128)}, f32[2,26,1,128]{3,1,2,0:T(8,128)}, u32[]{:S(2)}, u32[]{:S(2)}) collective-permute-start(f32[2,26,1,128]{3,1,2,0:T(8,128)} %get-tuple-element.60), channel_id=1, source_target_pairs={{0,1},{1,2},{2,3},{3,0},{4,5},{5,6},{6,7},{7,4},{8,9},{9,10},{10,1... | collective-permute-start | bytes 79880 | tf_op jit(solution)/shard_map/ppermute | solution.py:29
  173.8 58.2 %collective-permute-start.27 = (f32[2,26,1,128]{3,1,2,0:T(8,128)}, f32[2,26,1,128]{3,1,2,0:T(8,128)}, u32[]{:S(2)}, u32[]{:S(2)}) collective-permute-start(f32[2,26,1,128]{3,1,2,0:T(8,128)} %get-tuple-element.61), channel_id=1, source_target_pairs={{1,0},{2,1},{3,2},{0,3},{5,4},{6,5},{7,6},{4,7},{9,8},{10,9},{11,1... | collective-permute-start | bytes 79880 | tf_op jit(solution)/shard_map/ppermute | solution.py:32
  177.5 3.1 collective-permute-start.19
  221.1 3.7 collective-permute-start.20
  221.2 6.4 %collective-permute-start.21 = (f32[1,1,16,128]{3,2,1,0:T(8,128)S(1)}, f32[1,1,16,128]{3,2,1,0:T(8,128)S(1)}, u32[]{:S(2)}, u32[]{:S(2)}) collective-permute-start(f32[1,1,16,128]{3,2,1,0:T(8,128)S(1)} %get-tuple-element.86), channel_id=1, source_target_pairs={{0,4},{4,8},{8,12},{12,16},{16,20},{20,24},{24,28},{28,0},{1,5},{5... | collective-permute-start | bytes 24584 | tf_op jit(solution)/shard_map/ppermute | solution.py:29
  227.7 3.2 collective-permute-start.25
  236.3 14.2 %all-to-all-start = ((f32[4,2,12288]{2,1,0:T(2,128)}), f32[4,2,12288]{2,1,0:T(2,128)S(1)}, u32[]{:S(2)}, u32[]{:S(2)}) async-start(f32[4,2,12288]{2,1,0:T(2,128)} %fusion.110), calls=%async_computation | async-start | bytes 786432 | tf_op jit(solution)/shard_map/all_to_all | solution.py:260
  409.9 9.7 %all-to-all-start.1 = ((f32[4,2,6144]{2,1,0:T(2,128)}), f32[4,2,6144]{2,1,0:T(2,128)S(1)}, u32[]{:S(2)}, u32[]{:S(2)}) async-start(f32[4,2,6144]{2,1,0:T(2,128)} %all_to_all.13), calls=%async_computation.1 | async-start | bytes 393216 | tf_op jit(solution)/shard_map/all_to_all | solution.py:264
  (38 other events, 582.0 us)
